TPU v7x, 32 devices: a whole 2x2x4 slice. The times are simulated.
32 devices in a mesh: row: 4 (over x, core), col: 4 (over z), vir: 2 (over y).
Axes of the slice: x: 2, y: 2, z: 4, core: 2. Of those that a mesh axis runs over, the one named last changes fastest.
Arguments:
- amplitudes: float32 [80, 4, 4, 3, 128, 128], P('vir', 'row', 'col'), may hold values from -6 to 6
- integrals: float32 [80, 4, 4, 3, 128, 128], P('vir', 'row', 'col'), may hold values from -6 to 6
- cycle_terms: float32 [80, 4, 4, 3, 128, 128], P('vir', 'row', 'col'), may hold values from -0.15625 to 0.15625
- ladder_factors: float32 [80, 8, 128, 128], P('vir'), may hold values from -0.375 to 0.375
- live: int32 [80, 4, 4, 3], P('vir', 'row', 'col'), may hold values 0 or 1
Outputs:
- residual: float32 [80, 4, 4, 3, 128, 128], P('vir', 'row', 'col')
All inputs are finite; a program needn't handle non-finite values. No bound on the sum of `live` on one device may be relied on, other than what follows from the above.
Results may differ from a plain program's by a relative error of at most 0.0001.
Values sent between devices are 32-bit elements; how exact they have to be, the bound alone decides.
No kernel may reach another device: no remote copies, remote signals or barrier semaphores. Data moves between devices by JAX's collectives and lax.ppermute only.
A program may use at most 448 MiB of HBM per device.

v0:
```python
import jax
import jax.numpy as jnp
from jax import lax
from jax.sharding import PartitionSpec as P

NT = 80


def extended(block, sides, width):
    for axis, dim in sides:
        count = lax.axis_size(axis)
        forward = [(i, i + 1) for i in range(count - 1)]
        backward = [(target, source) for source, target in forward]
        low = lax.ppermute(
            lax.slice_in_dim(block, block.shape[dim] - width, None, axis=dim), axis, forward
        )
        high = lax.ppermute(lax.slice_in_dim(block, 0, width, axis=dim), axis, backward)
        block = jnp.concatenate([low, block, high], axis=dim)
    return block


def per_device(amplitudes, integrals, cycle_terms, ladder_factors, live):
    local_tiles = amplitudes.shape[0]
    occupied = amplitudes.shape[1]
    band_slots = amplitudes.shape[3]
    tile_size = amplitudes.shape[4]
    factor_count = ladder_factors.shape[1]
    half_band = band_slots // 2
    slot_index = jnp.arange(band_slots)
    global_rows = lax.axis_index("vir") * local_tiles + jnp.arange(local_tiles)
    col_tile = global_rows[:, None] + slot_index[None, :] - half_band
    inside = (col_tile >= 0) & (col_tile < NT)
    keep = ((live == 1) | (slot_index == half_band)[None, None, None, :]) & inside[:, None, None, :]
    keep_float = keep.astype(jnp.float32)[..., None, None]
    amps = amplitudes * keep_float
    pair_tiles = occupied * occupied * band_slots
    joined = jnp.concatenate(
        [cycle_terms.reshape(local_tiles, pair_tiles, tile_size, tile_size), ladder_factors], axis=1
    )
    widened = extended(joined, (("vir", 0),), half_band)
    cycle_ext = widened[:, :pair_tiles].reshape(
        local_tiles + 2 * half_band, occupied, occupied, band_slots, tile_size, tile_size
    )
    factors = widened[:, pair_tiles:]
    cycle_all = lax.all_gather(cycle_ext, "row", axis=1, tiled=True)
    centre = factors[half_band : half_band + local_tiles]
    ladder = jnp.zeros(amplitudes.shape, jnp.float32)
    for term_index in range(factor_count):
        inner = jnp.einsum(
            "axy,aijsyz->aijsxz", centre[:, term_index], amps, precision=lax.Precision.HIGHEST
        )
        parts = []
        for out_slot in range(band_slots):
            right_side = factors[out_slot : out_slot + local_tiles, term_index]
            parts.append(
                jnp.einsum(
                    "aijxz,awz->aijxw",
                    inner[:, :, :, out_slot],
                    right_side,
                    precision=lax.Precision.HIGHEST,
                )
            )
        ladder = ladder + jnp.stack(parts, axis=3)
    piece = lax.all_gather(amps, "col", axis=2, tiled=True)
    slot_sums = []
    for out_slot in range(band_slots):
        summed = jnp.zeros((local_tiles, occupied, occupied, tile_size, tile_size), jnp.float32)
        for in_slot in range(band_slots):
            mid_slot = out_slot - in_slot + half_band
            if 0 <= mid_slot < band_slots:
                cycle_rows = cycle_all[in_slot : in_slot + local_tiles, :, :, mid_slot]
                summed = summed + jnp.einsum(
                    "aiktu,akjuv->aijtv",
                    piece[:, :, :, in_slot],
                    cycle_rows,
                    precision=lax.Precision.HIGHEST,
                )
        slot_sums.append(summed)
    cycle = jnp.stack(slot_sums, axis=3)
    return keep_float * (integrals + ladder + cycle)


def solution(mesh):
    in_specs = (
        P("vir", "row", "col", None, None, None),
        P("vir", "row", "col", None, None, None),
        P("vir", "row", "col", None, None, None),
        P("vir", None, None, None),
        P("vir", "row", "col", None),
    )
    out_specs = P("vir", "row", "col", None, None, None)
    return jax.shard_map(
        per_device, mesh=mesh, in_specs=in_specs, out_specs=out_specs, check_vma=False
    )
```

profile of v0, /device:TPU:0, one launch (start us, length us, event | category | flops | bytes accessed | tf_op | source)
XLA Modules:
  0.0 918.6 jit_solution(8032832479250462117)
XLA Ops:
  27.4 14.0 %collective-permute-done = f32[1,11,128,128]{3,2,0,1:T(8,128)S(1)} collective-permute-done((f32[1,11,128,128]{3,2,0,1:T(8,128)S(1)}, f32[1,11,128,128]{3,2,0,1:T(8,128)S(1)}, u32[]{:S(2)}, u32[]{:S(2)}) %collective-permute-start) | collective-permute-done | bytes 720928 | tf_op jit(solution)/shard_map/ppermute | solution.py:14
  49.9 17.9 %fusion.32 = f32[40,1,1,3,128,128]{4,5,3,0,2,1:T(8,128)S(1)} fusion(f32[40,3]{0,1:T(4,128)S(1)} %bitcast.514, f32[40,1,1,3,128,128]{5,4,3,2,1,0:T(8,128)} %param.5, f32[40,8,128,128]{3,2,1,0:T(8,128)} %param.8), kind=kOutput, calls=%fused_computation.48 | convolution fusion | flops 3021864960 | bytes 18350560 | tf_op jit(solution)/shard_map/axy,aijsyz->aijsxz/dot_general | solution.py:49
  71.0 8.0 fusion.178
  79.1 18.1 %fusion.35 = f32[40,1,1,3,128,128]{4,5,3,0,2,1:T(8,128)} fusion(f32[40,3]{0,1:T(4,128)S(1)} %bitcast.515, f32[40,1,1,3,128,128]{5,4,3,2,1,0:T(8,128)} %param.5, f32[40,8,128,128]{3,2,1,0:T(8,128)} %param.8), kind=kOutput, calls=%fused_computation.49 | convolution fusion | flops 3021864960 | bytes 18350560 | tf_op jit(solution)/shard_map/axy,aijsyz->aijsxz/dot_general | solution.py:49
  104.9 15.8 %fusion.38 = f32[40,1,1,3,128,128]{4,5,3,0,2,1:T(8,128)} fusion(f32[40,3]{0,1:T(4,128)S(1)} %bitcast.516, f32[40,1,1,3,128,128]{5,4,3,2,1,0:T(8,128)S(1)} %bitcast.501, f32[40,8,128,128]{3,2,1,0:T(8,128)S(1)} %bitcast.499), kind=kOutput, calls=%fused_computation.50 | convolution fusion | flops 3021864960 | bytes 18352128 | tf_op jit(solution)/shard_map/axy,aijsyz->aijsxz/dot_general | solution.py:49
  128.3 15.5 %fusion.41 = f32[40,1,1,3,128,128]{4,5,3,0,2,1:T(8,128)} fusion(f32[40,3]{0,1:T(4,128)S(1)} %bitcast.517, f32[40,1,1,3,128,128]{5,4,3,2,1,0:T(8,128)S(1)} %bitcast.501, f32[40,8,128,128]{3,2,1,0:T(8,128)S(1)} %bitcast.499), kind=kOutput, calls=%fused_computation.51 | convolution fusion | flops 3021864960 | bytes 18352128 | tf_op jit(solution)/shard_map/axy,aijsyz->aijsxz/dot_general | solution.py:49
  151.6 15.6 %fusion.44 = f32[40,1,1,3,128,128]{4,5,3,0,2,1:T(8,128)} fusion(f32[40,3]{0,1:T(4,128)S(1)} %bitcast.518, f32[40,1,1,3,128,128]{5,4,3,2,1,0:T(8,128)S(1)} %bitcast.501, f32[40,8,128,128]{3,2,1,0:T(8,128)S(1)} %bitcast.499), kind=kOutput, calls=%fused_computation.52 | convolution fusion | flops 3021864960 | bytes 18352128 | tf_op jit(solution)/shard_map/axy,aijsyz->aijsxz/dot_general | solution.py:49
  174.9 15.9 %fusion.47 = f32[40,1,1,3,128,128]{4,5,3,0,2,1:T(8,128)} fusion(f32[40,3]{0,1:T(4,128)S(1)} %bitcast.519, f32[40,1,1,3,128,128]{5,4,3,2,1,0:T(8,128)S(1)} %bitcast.501, f32[40,8,128,128]{3,2,1,0:T(8,128)S(1)} %bitcast.499), kind=kOutput, calls=%fused_computation.53 | convolution fusion | flops 3021864960 | bytes 18352128 | tf_op jit(solution)/shard_map/axy,aijsyz->aijsxz/dot_general | solution.py:49
  198.5 15.6 %fusion.50 = f32[40,1,1,3,128,128]{4,5,3,0,2,1:T(8,128)} fusion(f32[40,3]{0,1:T(4,128)S(1)} %bitcast.520, f32[40,1,1,3,128,128]{5,4,3,2,1,0:T(8,128)S(1)} %bitcast.501, f32[40,8,128,128]{3,2,1,0:T(8,128)S(1)} %bitcast.499), kind=kOutput, calls=%fused_computation.54 | convolution fusion | flops 3021864960 | bytes 18352128 | tf_op jit(solution)/shard_map/axy,aijsyz->aijsxz/dot_general | solution.py:49
  221.9 18.1 %fusion.53 = f32[40,1,1,3,128,128]{4,5,3,0,2,1:T(8,128)} fusion(f32[40,3]{0,1:T(4,128)S(1)} %bitcast.521, f32[40,1,1,3,128,128]{5,4,3,2,1,0:T(8,128)} %param.5, f32[40,8,128,128]{3,2,1,0:T(8,128)S(1)} %bitcast.499), kind=kOutput, calls=%fused_computation.55 | convolution fusion | flops 3021864960 | bytes 18352128 | tf_op jit(solution)/shard_map/axy,aijsyz->aijsxz/dot_general | solution.py:49
  301.8 8.1 fusion.201
  363.9 8.1 fusion.181
  372.0 173.2 %all-gather.4.cloned.1.call-done = f32[40,1,4,3,128,128]{5,4,3,1,0,2:T(8,128)} async-done(((f32[40,1,1,3,128,128]{5,4,3,1,0,2:T(8,128)}), f32[40,1,4,3,128,128]{5,4,3,1,0,2:T(8,128)}) %all-gather.4.cloned.1.call-update) | async-done | bytes 31457296 | tf_op jit(solution)/shard_map/all_gather | solution.py:64
  545.2 25.9 %fusion.237 = (f32[40,1,4,1,128,128]{5,4,3,1,0,2:T(8,128)}, f32[40,1,4,1,128,128]{5,4,3,1,0,2:T(8,128)}, f32[40,1,4,1,128,128]{5,4,3,1,0,2:T(8,128)}) fusion(f32[40,1,4,3,128,128]{5,4,3,1,0,2:T(8,128)} %all-gather.4.cloned.1.call-done), kind=kLoop, calls=%fused_computation.267 | loop fusion | bytes 62914560 | tf_op jit(solution)/shard_map/slice | solution.py:74
  571.1 172.4 %all-gather.6.cloned.1.call-done = f32[42,12,128,128]{3,2,0,1:T(8,128)} async-done(((f32[42,3,128,128]{3,2,0,1:T(8,128)}), f32[42,12,128,128]{3,2,0,1:T(8,128)}) %all-gather.6.cloned.1.call-update) | async-done | bytes 33030160 | tf_op jit(solution)/shard_map/all_gather | solution.py:45
  743.6 24.3 %copy.172 = f32[42,12,128,128]{3,2,1,0:T(8,128)} copy(f32[42,12,128,128]{3,2,0,1:T(8,128)} %all-gather.6.cloned.1.call-done) | data formatting | bytes 66060288 | tf_op jit(solution)/shard_map/all_gather | solution.py:45
  768.2 15.4 %fusion.4 = f32[40,128,128,1]{1,2,3,0:T(8,128)} fusion(f32[42,4,1,3,128,128]{5,4,3,1,0,2:T(8,128)} %bitcast.502, f32[40,1,4,1,128,128]{5,4,3,1,0,2:T(8,128)S(1)} %copy-done.1), kind=kOutput, calls=%fused_computation.9 | convolution fusion | flops 4026531840 | bytes 23592960 | tf_op jit(solution)/shard_map/aiktu,akjuv->aijtv/dot_general | solution.py:72
  783.6 16.2 %fusion.6 = f32[40,128,128,1]{1,2,3,0:T(8,128)S(1)} fusion(f32[42,4,1,3,128,128]{5,4,3,1,0,2:T(8,128)} %bitcast.503, f32[40,1,4,1,128,128]{5,4,3,1,0,2:T(8,128)} %get-tuple-element.5), kind=kOutput, calls=%fused_computation.13 | convolution fusion | flops 4026531840 | bytes 23592960 | tf_op jit(solution)/shard_map/aiktu,akjuv->aijtv/dot_general | solution.py:72
  799.9 15.3 %fusion.3 = f32[40,128,128,1]{1,2,3,0:T(8,128)} fusion(f32[42,4,1,3,128,128]{5,4,3,1,0,2:T(8,128)} %bitcast.504, f32[40,1,4,1,128,128]{5,4,3,1,0,2:T(8,128)S(1)} %bitcast.510), kind=kOutput, calls=%fused_computation.7 | convolution fusion | flops 4026531840 | bytes 23592960 | tf_op jit(solution)/shard_map/aiktu,akjuv->aijtv/dot_general | solution.py:72
  815.2 15.4 %fusion.1 = f32[40,128,128,1]{1,2,3,0:T(8,128)} fusion(f32[42,4,1,3,128,128]{5,4,3,1,0,2:T(8,128)} %bitcast.505, f32[40,1,4,1,128,128]{5,4,3,1,0,2:T(8,128)S(1)} %bitcast.510), kind=kOutput, calls=%fused_computation.3 | convolution fusion | flops 4026531840 | bytes 23592960 | tf_op jit(solution)/shard_map/aiktu,akjuv->aijtv/dot_general | solution.py:72
  830.6 15.6 %fusion.152 = f32[40,1,1,1,128,128]{5,4,0,3,2,1:T(8,128)} fusion(f32[40,128,128,1]{1,2,3,0:T(8,128)S(1)} %fusion.6, f32[40,1,4,1,128,128]{5,4,3,1,0,2:T(8,128)S(1)} %bitcast.510, f32[42,4,1,3,128,128]{5,4,3,1,0,2:T(8,128)} %bitcast.506), kind=kOutput, calls=%fused_computation.196 | convolution fusion | flops 4027187200 | bytes 26214400 | tf_op jit(solution)/shard_map/aiktu,akjuv->aijtv/dot_general | solution.py:72
  846.2 20.5 %fusion.150 = f32[40,1,1,1,128,128]{5,4,0,3,2,1:T(8,128)} fusion(f32[40,128,128,1]{1,2,3,0:T(8,128)} %fusion.1, f32[40,1,4,1,128,128]{5,4,3,1,0,2:T(8,128)} %get-tuple-element.7, f32[42,4,1,3,128,128]{5,4,3,1,0,2:T(8,128)} %bitcast.507), kind=kOutput, calls=%fused_computation.191 | convolution fusion | flops 4027187200 | bytes 26214400 | tf_op jit(solution)/shard_map/aiktu,akjuv->aijtv/dot_general | solution.py:72
  866.7 16.1 %fusion.151 = f32[40,1,1,1,128,128]{5,4,0,3,2,1:T(8,128)} fusion(f32[40,128,128,1]{1,2,3,0:T(8,128)} %fusion.3, f32[40,128,128,1]{1,2,3,0:T(8,128)S(1)} %copy-done.4, f32[40,1,4,1,128,128]{5,4,3,1,0,2:T(8,128)S(1)} %bitcast.512, f32[42,4,1,3,128,128]{5,4,3,1,0,2:T(8,128)} %bitcast.508), kind=kOutput, calls=%fused_computation.193 | convolution fusion | flops 4027842560 | bytes 28835840 | tf_op jit(solution)/shard_map/aiktu,akjuv->aijtv/dot_general | solution.py:72
  882.9 25.0 %fusion.15 = f32[40,1,1,3,128,128]{5,4,0,3,2,1:T(8,128)S(1)} fusion(f32[40,1,1,1,128,128]{5,4,0,3,2,1:T(8,128)} %fusion.181, f32[40,1,1,1,128,128]{5,4,0,3,2,1:T(8,128)} %fusion.178, f32[40,1,1,1,128,128]{5,4,0,3,2,1:T(8,128)} %fusion.177, f32[40,1,1,1,128,128]{5,4,0,3,2,1:T(8,128)} %fusion.186, f32[40,1,1,1,128,128]{5,4,0,3,2,1:T(8,128)} %fusion.183, ...), kind=kLoop, calls=%fused_computation.29 | loop fusion | flops 55050240 | bytes 86508000 | tf_op jit(solution)/shard_map/mul | solution.py:80
  (87 shorter events, 198.8 us)
Async XLA Ops:
  6.5 538.7 %all-gather.4.cloned.1.call-start = ((), (), s32[]{:S(2)}) async-start(), calls=%async_computation | async-start | bytes 39321600 | tf_op jit(solution)/shard_map/all_gather | solution.py:64
  7.3 214.6 %copy-start.5 = (f32[40,1,1,3]{0,3,2,1:T(4,128)}, f32[40,1,1,3]{0,3,2,1:T(4,128)S(1)}, u32[]{:S(2)}) copy-start(f32[40,1,1,3]{0,3,2,1:T(4,128)S(1)} %copy.436) | copy-start | bytes 1444
  15.3 728.3 %all-gather.6.cloned.1.call-start = ((), (), s32[]{:S(2)}) async-start(), calls=%async_computation.1 | async-start | bytes 41287680 | tf_op jit(solution)/shard_map/all_gather | solution.py:45
  19.1 26.5 %copy-start = (f32[40,1,1,3,128,128]{5,4,0,3,2,1:T(8,128)}, f32[40,1,1,3,128,128]{5,4,0,3,2,1:T(8,128)S(1)}, u32[]{:S(2)}) copy-start(f32[40,1,1,3,128,128]{5,4,0,3,2,1:T(8,128)S(1)} %copy.435) | copy-start | bytes 23592964
  21.2 20.3 %collective-permute-start = (f32[1,11,128,128]{3,2,0,1:T(8,128)S(1)}, f32[1,11,128,128]{3,2,0,1:T(8,128)S(1)}, u32[]{:S(2)}, u32[]{:S(2)}) collective-permute-start(f32[1,11,128,128]{3,2,0,1:T(8,128)S(1)} %get-tuple-element.8), channel_id=1, source_target_pairs={{0,1},{2,3},{4,5},{6,7},{8,9},{10,11},{12,13},{14,15},{16,17},{18,... | collective-permute-start | bytes 2162696 | tf_op jit(solution)/shard_map/ppermute | solution.py:14
  26.1 19.5 %collective-permute-start.1 = (f32[1,11,128,128]{3,2,0,1:T(8,128)S(1)}, f32[1,11,128,128]{3,2,0,1:T(8,128)S(1)}, u32[]{:S(2)}, u32[]{:S(2)}) collective-permute-start(f32[1,11,128,128]{3,2,0,1:T(8,128)S(1)} %get-tuple-element.9), channel_id=1, source_target_pairs={{1,0},{3,2},{5,4},{7,6},{9,8},{11,10},{13,12},{15,14},{17,16},{19,... | collective-permute-start | bytes 2162696 | tf_op jit(solution)/shard_map/ppermute | solution.py:17
  49.9 47.3 %slice-start.2 = ((s8[20971520]{0:T(1024)(128)(4,1)}), s8[4194304]{0:T(1024)(128)(4,1)S(1)}, s32[]{:S(2)}) async-start(s8[20971520]{0:T(1024)(128)(4,1)} %bitcast.498), calls=%async_computation.4 | async-start | bytes 8388608
  49.9 47.3 %slice-start.3 = ((s8[20971520]{0:T(1024)(128)(4,1)}), s8[4194304]{0:T(1024)(128)(4,1)S(1)}, s32[]{:S(2)}) async-start(s8[20971520]{0:T(1024)(128)(4,1)} %bitcast.498), calls=%async_computation.5 | async-start | bytes 8388608
  49.9 47.3 %slice-start.4 = ((s8[20971520]{0:T(1024)(128)(4,1)}), s8[4194304]{0:T(1024)(128)(4,1)S(1)}, s32[]{:S(2)}) async-start(s8[20971520]{0:T(1024)(128)(4,1)} %bitcast.498), calls=%async_computation.6 | async-start | bytes 8388608
  71.0 33.9 %slice-start.7 = ((s8[7864320]{0:T(1024)(128)(4,1)}), s8[4194304]{0:T(1024)(128)(4,1)S(1)}, s32[]{:S(2)}) async-start(s8[7864320]{0:T(1024)(128)(4,1)} %bitcast.500), calls=%async_computation.9 | async-start | bytes 8388608
  79.1 18.1 %slice-start.5 = ((s8[20971520]{0:T(1024)(128)(4,1)}), s8[4194304]{0:T(1024)(128)(4,1)S(1)}, s32[]{:S(2)}) async-start(s8[20971520]{0:T(1024)(128)(4,1)} %bitcast.498), calls=%async_computation.7 | async-start | bytes 8388608
  79.1 18.2 %slice-start.6 = ((s8[20971520]{0:T(1024)(128)(4,1)}), s8[4194304]{0:T(1024)(128)(4,1)S(1)}, s32[]{:S(2)}) async-start(s8[20971520]{0:T(1024)(128)(4,1)} %bitcast.498), calls=%async_computation.8 | async-start | bytes 8388608
  79.1 25.8 %slice-start.8 = ((s8[7864320]{0:T(1024)(128)(4,1)}), s8[3670016]{0:T(1024)(128)(4,1)S(1)}, s32[]{:S(2)}) async-start(s8[7864320]{0:T(1024)(128)(4,1)} %bitcast.500), calls=%async_computation.10 | async-start | bytes 7340032
  214.0 33.6 %slice-start = ((s8[7864320]{0:T(1024)(128)(4,1)}), s8[4194304]{0:T(1024)(128)(4,1)S(1)}, s32[]{:S(2)}) async-start(s8[7864320]{0:T(1024)(128)(4,1)} %bitcast.480), calls=%async_computation.2 | async-start | bytes 8388608
  221.9 25.7 %slice-start.1 = ((s8[7864320]{0:T(1024)(128)(4,1)}), s8[3670016]{0:T(1024)(128)(4,1)S(1)}, s32[]{:S(2)}) async-start(s8[7864320]{0:T(1024)(128)(4,1)} %bitcast.480), calls=%async_computation.3 | async-start | bytes 7340032
  743.6 24.7 %copy-start.1 = (f32[40,1,4,1,128,128]{5,4,3,1,0,2:T(8,128)S(1)}, f32[40,1,4,1,128,128]{5,4,3,1,0,2:T(8,128)}, u32[]{:S(2)}) copy-start(f32[40,1,4,1,128,128]{5,4,3,1,0,2:T(8,128)} %get-tuple-element.5) | copy-start | bytes 31457284
  768.2 31.7 %slice-start.9 = ((s8[10485760]{0:T(1024)(128)(4,1)}), s8[4194304]{0:T(1024)(128)(4,1)S(1)}, s32[]{:S(2)}) async-start(s8[10485760]{0:T(1024)(128)(4,1)} %bitcast.509), calls=%async_computation.11 | async-start | bytes 8388608
  768.2 31.7 %slice-start.10 = ((s8[10485760]{0:T(1024)(128)(4,1)}), s8[4194304]{0:T(1024)(128)(4,1)S(1)}, s32[]{:S(2)}) async-start(s8[10485760]{0:T(1024)(128)(4,1)} %bitcast.509), calls=%async_computation.12 | async-start | bytes 8388608
  783.6 16.3 %slice-start.11 = ((s8[10485760]{0:T(1024)(128)(4,1)}), s8[2097152]{0:T(1024)(128)(4,1)S(1)}, s32[]{:S(2)}) async-start(s8[10485760]{0:T(1024)(128)(4,1)} %bitcast.509), calls=%async_computation.13 | async-start | bytes 4194304
  830.6 36.1 %slice-start.12 = ((s8[10485760]{0:T(1024)(128)(4,1)}), s8[2097152]{0:T(1024)(128)(4,1)S(1)}, s32[]{:S(2)}) async-start(s8[10485760]{0:T(1024)(128)(4,1)} %bitcast.511), calls=%async_computation.14 | async-start | bytes 4194304
  830.6 36.1 %slice-start.13 = ((s8[10485760]{0:T(1024)(128)(4,1)}), s8[4194304]{0:T(1024)(128)(4,1)S(1)}, s32[]{:S(2)}) async-start(s8[10485760]{0:T(1024)(128)(4,1)} %bitcast.511), calls=%async_computation.15 | async-start | bytes 8388608
  846.2 20.5 %slice-start.14 = ((s8[10485760]{0:T(1024)(128)(4,1)}), s8[4194304]{0:T(1024)(128)(4,1)S(1)}, s32[]{:S(2)}) async-start(s8[10485760]{0:T(1024)(128)(4,1)} %bitcast.511), calls=%async_computation.16 | async-start | bytes 8388608
  846.2 20.5 %copy-start.4 = (f32[40,128,128,1]{1,2,3,0:T(8,128)S(1)}, f32[40,128,128,1]{1,2,3,0:T(8,128)}, u32[]{:S(2)}) copy-start(f32[40,128,128,1]{1,2,3,0:T(8,128)} %fusion.4) | copy-start | bytes 7864324
  866.7 16.2 %copy-start.3 = (f32[40,1,1,1,128,128]{5,4,0,3,2,1:T(8,128)S(1)}, f32[40,1,1,1,128,128]{5,4,0,3,2,1:T(8,128)}, u32[]{:S(2)}) copy-start(f32[40,1,1,1,128,128]{5,4,0,3,2,1:T(8,128)} %fusion.182) | copy-start | bytes 7864324
  (2 other events, 19.4 us)
Sparse Core Ops, SparseCore 0:
  15.4 529.8 all-gather.3
  546.8 196.6 all-gather.5
where the time goes:
time: 922 us; the launch traced here: 919 us
  matrix products  433 us (47%)
  waiting for transfers between devices  364 us (39%)
  local copies, waits for them, and re-layouts  65.5 us (7%)
  other arithmetic  35.8 us (4%)
  between operations  13.8 us (1%)
    dot_general x24, matrix products, per_device(): jnp.einsum('aijxz,awz->aijxw', inner[:, :, :, out_slot], right_side, prec...  186 us
    all_gather x1, waiting for transfers between devices, per_device(): piece = lax.all_gather(amps, 'col', axis=2, tiled=True)  173 us
    all_gather x1, waiting for transfers between devices, per_device(): cycle_all = lax.all_gather(cycle_ext, 'row', axis=1, tiled=True)  172 us
    dot_general x8, matrix products, per_device(): jnp.einsum('axy,aijsyz->aijsxz', centre[:, term_index], amps, precision=l...  132 us
    dot_general x7, matrix products, per_device(): jnp.einsum('aiktu,akjuv->aijtv', piece[:, :, :, in_slot], cycle_rows, pre...  115 us
    slice x1, local copies, waits for them, and re-layouts, per_device(): piece[:, :, :, in_slot]  25.9 us
    mul x2, other arithmetic, per_device(): return keep_float * (integrals + ladder + cycle)  25.7 us
    all_gather x1, local copies, waits for them, and re-layouts, per_device(): cycle_all = lax.all_gather(cycle_ext, 'row', axis=1, tiled=True)  24.3 us
  transfers between devices with their start and end apart: 4, of which 4 were waited for; matrix products, arithmetic and copies ran while one was open for 39% of the time, Pallas kernels for 0%

commit v1 on v0

--- a/solution.py
+++ b/solution.py
@@ -42,7 +42,25 @@
         local_tiles + 2 * half_band, occupied, occupied, band_slots, tile_size, tile_size
     )
     factors = widened[:, pair_tiles:]
-    cycle_all = lax.all_gather(cycle_ext, "row", axis=1, tiled=True)
+    peers, place, rows = (lax.axis_size("row"), lax.axis_index("row"), cycle_ext.shape[1])
+    ahead = [(i_2, (i_2 + 1) % peers) for i_2 in range(peers)]
+    downward = [(i_2, (i_2 - 1) % peers) for i_2 in range(peers)]
+    cycle_all = jnp.zeros(
+        (*cycle_ext.shape[:1], peers * rows, *cycle_ext.shape[1 + 1 :]), cycle_ext.dtype
+    )
+    cycle_all = lax.dynamic_update_slice_in_dim(cycle_all, cycle_ext, place * rows, axis=1)
+    from_left = from_right = cycle_ext
+    half = peers // 2
+    for step in range(1, half + 1):
+        from_left = lax.ppermute(from_left, "row", ahead)
+        cycle_all = lax.dynamic_update_slice_in_dim(
+            cycle_all, from_left, (place - step) % peers * rows, axis=1
+        )
+        if step < peers - half:
+            from_right = lax.ppermute(from_right, "row", downward)
+            cycle_all = lax.dynamic_update_slice_in_dim(
+                cycle_all, from_right, (place + step) % peers * rows, axis=1
+            )
     centre = factors[half_band : half_band + local_tiles]
     ladder = jnp.zeros(amplitudes.shape, jnp.float32)
     for term_index in range(factor_count):

time: 922 us -> 713 us (0.77)
  waiting for transfers between devices: 364 us -> 113 us
  local copies, waits for them, and re-layouts: 65.5 us -> 112 us
    all_gather x1 -> x0, waiting for transfers between devices: 172 us -> none  [per_device(): cycle_all = lax.all_gather(cycle_ext, 'row', axis=1, tiled=True)]
    all_gather x1, waiting for transfers between devices: 173 us -> 94.6 us  [per_device(): piece = lax.all_gather(amps, 'col', axis=2, tiled=True)]
    dynamic_update_slice x0 -> x4, local copies, waits for them, and re-layouts: none -> 27.5 us  [the longest x2 15.4 us: per_device(): lax.dynamic_update_slice_in_dim(cycle_all, from_left, (place - step) % pe...]
    ppermute x0 -> x3, local copies, waits for them, and re-layouts: none -> 26.7 us  [the longest x2 17.7 us: per_device(): from_left = lax.ppermute(from_left, 'row', ahead)]
    all_gather x1 -> x0, local copies, waits for them, and re-layouts: 24.3 us -> none  [per_device(): cycle_all = lax.all_gather(cycle_ext, 'row', axis=1, tiled=True)]
    broadcast_in_dim x0 -> x1, local copies, waits for them, and re-layouts: none -> 16.7 us  [per_device(): jnp.zeros((*cycle_ext.shape[:1], peers * rows, *cycle_ext.shape[1 + 1:]),...]
  transfers between devices with their start and end apart: 4 -> 6, of which waited for: 4 -> 3; matrix products, arithmetic and copies ran while one was open for 39% -> 57% of each run, Pallas kernels for 0% -> 0%
where the time goes in v1:
time: 713 us; the launch traced here: 709 us
  matrix products  425 us (60%)
  waiting for transfers between devices  113 us (16%)
  local copies, waits for them, and re-layouts  112 us (16%)
  other arithmetic  35.6 us (5%)
  between operations  14.2 us (2%)
  starting transfers between devices  8.55 us (1%)
    dot_general x24, matrix products, per_device(): jnp.einsum('aijxz,awz->aijxw', inner[:, :, :, out_slot], right_side, prec...  186 us
    dot_general x8, matrix products, per_device(): jnp.einsum('axy,aijsyz->aijsxz', centre[:, term_index], amps, precision=l...  130 us
    dot_general x7, matrix products, per_device(): jnp.einsum('aiktu,akjuv->aijtv', piece[:, :, :, in_slot], cycle_rows, pre...  110 us
    all_gather x1, waiting for transfers between devices, per_device(): piece = lax.all_gather(amps, 'col', axis=2, tiled=True)  94.6 us
    mul x2, other arithmetic, per_device(): return keep_float * (integrals + ladder + cycle)  25.9 us
    ppermute x2, local copies, waits for them, and re-layouts, per_device(): from_left = lax.ppermute(from_left, 'row', ahead)  17.7 us
    slice x1, local copies, waits for them, and re-layouts, per_device(): piece[:, :, :, in_slot]  17.7 us
    broadcast_in_dim x1, local copies, waits for them, and re-layouts, per_device(): jnp.zeros((*cycle_ext.shape[:1], peers * rows, *cycle_ext.shape[1 + 1:]),...  16.7 us
  transfers between devices with their start and end apart: 6, of which 3 were waited for; matrix products, arithmetic and copies ran while one was open for 57% of the time, Pallas kernels for 0%

profile of v1, /device:TPU:0, one launch (start us, length us, event | category | flops | bytes accessed | tf_op | source)
XLA Modules:
  0.0 708.9 jit_solution(1353809689329687328)
XLA Ops:
  27.4 14.0 %collective-permute-done = f32[1,11,128,128]{3,2,0,1:T(8,128)S(1)} collective-permute-done((f32[1,11,128,128]{3,2,0,1:T(8,128)S(1)}, f32[1,11,128,128]{3,2,0,1:T(8,128)S(1)}, u32[]{:S(2)}, u32[]{:S(2)}) %collective-permute-start) | collective-permute-done | bytes 720928 | tf_op jit(solution)/shard_map/ppermute | solution.py:14
  49.9 17.8 %fusion.33 = f32[40,1,1,3,128,128]{4,5,3,0,2,1:T(8,128)S(1)} fusion(f32[40,3]{0,1:T(4,128)S(1)} %bitcast.501, f32[40,1,1,3,128,128]{5,4,3,2,1,0:T(8,128)} %param.5, f32[40,8,128,128]{3,2,1,0:T(8,128)} %param.8), kind=kOutput, calls=%fused_computation.49 | convolution fusion | flops 3021864960 | bytes 18350560 | tf_op jit(solution)/shard_map/axy,aijsyz->aijsxz/dot_general | solution.py:67
  78.7 18.0 %fusion.36 = f32[40,1,1,3,128,128]{4,5,3,0,2,1:T(8,128)} fusion(f32[40,3]{0,1:T(4,128)S(1)} %bitcast.502, f32[40,1,1,3,128,128]{5,4,3,2,1,0:T(8,128)} %param.5, f32[40,8,128,128]{3,2,1,0:T(8,128)} %param.8), kind=kOutput, calls=%fused_computation.50 | convolution fusion | flops 3021864960 | bytes 18350560 | tf_op jit(solution)/shard_map/axy,aijsyz->aijsxz/dot_general | solution.py:67
  104.5 15.8 %fusion.39 = f32[40,1,1,3,128,128]{4,5,3,0,2,1:T(8,128)} fusion(f32[40,3]{0,1:T(4,128)S(1)} %bitcast.503, f32[40,1,1,3,128,128]{5,4,3,2,1,0:T(8,128)S(1)} %bitcast.497, f32[40,8,128,128]{3,2,1,0:T(8,128)S(1)} %bitcast.493), kind=kOutput, calls=%fused_computation.51 | convolution fusion | flops 3021864960 | bytes 18352128 | tf_op jit(solution)/shard_map/axy,aijsyz->aijsxz/dot_general | solution.py:67
  128.0 15.6 %fusion.42 = f32[40,1,1,3,128,128]{4,5,3,0,2,1:T(8,128)} fusion(f32[40,3]{0,1:T(4,128)S(1)} %bitcast.504, f32[40,1,1,3,128,128]{5,4,3,2,1,0:T(8,128)S(1)} %bitcast.497, f32[40,8,128,128]{3,2,1,0:T(8,128)S(1)} %bitcast.493), kind=kOutput, calls=%fused_computation.52 | convolution fusion | flops 3021864960 | bytes 18352128 | tf_op jit(solution)/shard_map/axy,aijsyz->aijsxz/dot_general | solution.py:67
  151.3 15.6 %fusion.45 = f32[40,1,1,3,128,128]{4,5,3,0,2,1:T(8,128)} fusion(f32[40,3]{0,1:T(4,128)S(1)} %bitcast.505, f32[40,1,1,3,128,128]{5,4,3,2,1,0:T(8,128)S(1)} %bitcast.497, f32[40,8,128,128]{3,2,1,0:T(8,128)S(1)} %bitcast.493), kind=kOutput, calls=%fused_computation.53 | convolution fusion | flops 3021864960 | bytes 18352128 | tf_op jit(solution)/shard_map/axy,aijsyz->aijsxz/dot_general | solution.py:67
  174.5 15.6 %fusion.48 = f32[40,1,1,3,128,128]{4,5,3,0,2,1:T(8,128)} fusion(f32[40,3]{0,1:T(4,128)S(1)} %bitcast.506, f32[40,1,1,3,128,128]{5,4,3,2,1,0:T(8,128)S(1)} %bitcast.497, f32[40,8,128,128]{3,2,1,0:T(8,128)S(1)} %bitcast.493), kind=kOutput, calls=%fused_computation.54 | convolution fusion | flops 3021864960 | bytes 18352128 | tf_op jit(solution)/shard_map/axy,aijsyz->aijsxz/dot_general | solution.py:67
  191.8 15.8 %fusion.51 = f32[40,1,1,3,128,128]{4,5,3,0,2,1:T(8,128)} fusion(f32[40,3]{0,1:T(4,128)S(1)} %bitcast.507, f32[40,1,1,3,128,128]{5,4,3,2,1,0:T(8,128)S(1)} %bitcast.497, f32[40,8,128,128]{3,2,1,0:T(8,128)S(1)} %bitcast.493), kind=kOutput, calls=%fused_computation.55 | convolution fusion | flops 3021864960 | bytes 18352128 | tf_op jit(solution)/shard_map/axy,aijsyz->aijsxz/dot_general | solution.py:67
  223.1 15.7 %fusion.54 = f32[40,1,1,3,128,128]{4,5,3,0,2,1:T(8,128)} fusion(f32[40,3]{0,1:T(4,128)S(1)} %bitcast.508, f32[40,1,1,3,128,128]{5,4,3,2,1,0:T(8,128)S(1)} %bitcast.497, f32[40,8,128,128]{3,2,1,0:T(8,128)S(1)} %bitcast.493), kind=kOutput, calls=%fused_computation.56 | convolution fusion | flops 3021864960 | bytes 18352128 | tf_op jit(solution)/shard_map/axy,aijsyz->aijsxz/dot_general | solution.py:67
  246.6 8.9 %copy.113 = f32[42,1,1,3,128,128]{4,5,1,0,3,2:T(8,128)} copy(f32[42,1,1,3,128,128]{5,4,0,3,2,1:T(8,128)} %fusion.7) | data formatting | bytes 16515072 | tf_op jit(solution)/shard_map/reshape | solution.py:41
  255.5 16.7 %broadcast_in_dim.2 = f32[42,4,1,3,128,128]{4,5,1,0,3,2:T(8,128)} broadcast(f32[]{:T(128)} %constant.44.clone.1), dimensions={} | broadcast | bytes 33030148 | tf_op jit(solution)/shard_map/broadcast_in_dim | solution.py:48
  404.2 8.9 %copy.114 = f32[42,1,1,3,128,128]{4,5,1,0,3,2:T(8,128)} copy(f32[42,1,1,3,128,128]{5,4,0,3,2,1:T(8,128)} %collective-permute-done.2) | data formatting | bytes 16515072 | tf_op jit(solution)/shard_map/ppermute | solution.py:55
  413.1 9.0 %copy.115 = f32[42,1,1,3,128,128]{4,5,1,0,3,2:T(8,128)} copy(f32[42,1,1,3,128,128]{5,4,0,3,2,1:T(8,128)} %collective-permute-done.3) | data formatting | bytes 16515072 | tf_op jit(solution)/shard_map/ppermute | solution.py:60
  434.0 8.9 %copy.116 = f32[42,1,1,3,128,128]{4,5,1,0,3,2:T(8,128)} copy(f32[42,1,1,3,128,128]{5,4,0,3,2,1:T(8,128)} %collective-permute-done.4) | data formatting | bytes 16515072 | tf_op jit(solution)/shard_map/ppermute | solution.py:55
  450.6 94.6 %all-gather.2.cloned.1.call-done = f32[40,1,4,3,128,128]{5,4,3,1,0,2:T(8,128)} async-done(((f32[40,1,1,3,128,128]{5,4,3,1,0,2:T(8,128)}), f32[40,1,4,3,128,128]{5,4,3,1,0,2:T(8,128)}) %all-gather.2.cloned.1.call-update) | async-done | bytes 31457296 | tf_op jit(solution)/shard_map/all_gather | solution.py:82
  545.2 17.7 %fusion.238 = (f32[40,1,4,1,128,128]{5,4,3,1,0,2:T(8,128)}, f32[40,1,4,1,128,128]{5,4,3,1,0,2:T(8,128)S(1)}, f32[40,1,4,1,128,128]{5,4,3,1,0,2:T(8,128)}) fusion(f32[40,1,4,3,128,128]{5,4,3,1,0,2:T(8,128)} %all-gather.2.cloned.1.call-done), kind=kLoop, calls=%fused_computation.272 | loop fusion | bytes 62914560 | tf_op jit(solution)/shard_map/slice | solution.py:92
  562.9 14.6 %fusion.6 = f32[40,128,128,1]{1,2,3,0:T(8,128)S(1)} fusion(f32[42,4,1,3,128,128]{4,5,1,0,3,2:T(8,128)} %constant_dynamic-update-slice_fusion, f32[40,1,4,1,128,128]{5,4,3,1,0,2:T(8,128)} %get-tuple-element.5), kind=kOutput, calls=%fused_computation.13 | convolution fusion | flops 4026531840 | bytes 23592960 | tf_op jit(solution)/shard_map/aiktu,akjuv->aijtv/dot_general | solution.py:90
  577.5 16.4 %fusion.4 = f32[40,128,128,1]{1,2,3,0:T(8,128)} fusion(f32[42,4,1,3,128,128]{4,5,1,0,3,2:T(8,128)} %constant_dynamic-update-slice_fusion, f32[40,1,4,1,128,128]{5,4,3,1,0,2:T(8,128)} %get-tuple-element.5), kind=kOutput, calls=%fused_computation.9 | convolution fusion | flops 4026531840 | bytes 23592960 | tf_op jit(solution)/shard_map/aiktu,akjuv->aijtv/dot_general | solution.py:90
  593.9 14.5 %fusion.3 = f32[40,128,128,1]{1,2,3,0:T(8,128)} fusion(f32[42,4,1,3,128,128]{4,5,1,0,3,2:T(8,128)} %constant_dynamic-update-slice_fusion, f32[40,1,4,1,128,128]{5,4,3,1,0,2:T(8,128)S(1)} %get-tuple-element.6), kind=kOutput, calls=%fused_computation.7 | convolution fusion | flops 4026531840 | bytes 23592960 | tf_op jit(solution)/shard_map/aiktu,akjuv->aijtv/dot_general | solution.py:90
  608.5 14.6 %fusion.1 = f32[40,128,128,1]{1,2,3,0:T(8,128)} fusion(f32[42,4,1,3,128,128]{4,5,1,0,3,2:T(8,128)} %constant_dynamic-update-slice_fusion, f32[40,1,4,1,128,128]{5,4,3,1,0,2:T(8,128)S(1)} %get-tuple-element.6), kind=kOutput, calls=%fused_computation.3 | convolution fusion | flops 4026531840 | bytes 23592960 | tf_op jit(solution)/shard_map/aiktu,akjuv->aijtv/dot_general | solution.py:90
  623.1 14.7 %fusion.153 = f32[40,1,1,1,128,128]{5,4,0,3,2,1:T(8,128)} fusion(f32[40,128,128,1]{1,2,3,0:T(8,128)S(1)} %fusion.6, f32[40,1,4,1,128,128]{5,4,3,1,0,2:T(8,128)S(1)} %get-tuple-element.6, f32[42,4,1,3,128,128]{4,5,1,0,3,2:T(8,128)} %constant_dynamic-update-slice_fusion), kind=kOutput, calls=%fused_computation.197 | convolution fusion | flops 4027187200 | bytes 26214400 | tf_op jit(solution)/shard_map/aiktu,akjuv->aijtv/dot_general | solution.py:90
  637.8 19.4 %fusion.151 = f32[40,1,1,1,128,128]{5,4,0,3,2,1:T(8,128)} fusion(f32[40,128,128,1]{1,2,3,0:T(8,128)} %fusion.1, f32[40,1,4,1,128,128]{5,4,3,1,0,2:T(8,128)} %get-tuple-element.7, f32[42,4,1,3,128,128]{4,5,1,0,3,2:T(8,128)} %constant_dynamic-update-slice_fusion), kind=kOutput, calls=%fused_computation.192 | convolution fusion | flops 4027187200 | bytes 26214400 | tf_op jit(solution)/shard_map/aiktu,akjuv->aijtv/dot_general | solution.py:90
  657.3 15.3 %fusion.152 = f32[40,1,1,1,128,128]{5,4,0,3,2,1:T(8,128)} fusion(f32[40,128,128,1]{1,2,3,0:T(8,128)} %fusion.3, f32[40,128,128,1]{1,2,3,0:T(8,128)S(1)} %copy-done.4, f32[40,1,4,1,128,128]{5,4,3,1,0,2:T(8,128)S(1)} %bitcast.499, f32[42,4,1,3,128,128]{4,5,1,0,3,2:T(8,128)} %constant_dynamic-update-slice_fusion), kind=kOutput, calls=%fused_computation.194 | convolution fusion | flops 4027842560 | bytes 28835840 | tf_op jit(solution)/shard_map/aiktu,akjuv->aijtv/dot_general | solution.py:90
  672.6 25.2 %fusion.16 = f32[40,1,1,3,128,128]{5,4,0,3,2,1:T(8,128)S(1)} fusion(f32[40,1,1,1,128,128]{5,4,0,3,2,1:T(8,128)} %fusion.182, f32[40,1,1,1,128,128]{5,4,0,3,2,1:T(8,128)} %fusion.179, f32[40,1,1,1,128,128]{5,4,0,3,2,1:T(8,128)} %fusion.178, f32[40,1,1,1,128,128]{5,4,0,3,2,1:T(8,128)} %fusion.187, f32[40,1,1,1,128,128]{5,4,0,3,2,1:T(8,128)} %fusion.184, ...), kind=kLoop, calls=%fused_computation.30 | loop fusion | flops 55050240 | bytes 86508000 | tf_op jit(solution)/shard_map/mul | solution.py:98
  (102 shorter events, 251.2 us)
Async XLA Ops:
  6.5 538.7 %all-gather.2.cloned.1.call-start = ((), (), s32[]{:S(2)}) async-start(), calls=%async_computation | async-start | bytes 39321600 | tf_op jit(solution)/shard_map/all_gather | solution.py:82
  7.3 215.8 %copy-start.5 = (f32[40,1,1,3]{0,3,2,1:T(4,128)}, f32[40,1,1,3]{0,3,2,1:T(4,128)S(1)}, u32[]{:S(2)}) copy-start(f32[40,1,1,3]{0,3,2,1:T(4,128)S(1)} %copy.366) | copy-start | bytes 1444
  19.0 26.5 %copy-start = (f32[40,1,1,3,128,128]{5,4,0,3,2,1:T(8,128)}, f32[40,1,1,3,128,128]{5,4,0,3,2,1:T(8,128)S(1)}, u32[]{:S(2)}) copy-start(f32[40,1,1,3,128,128]{5,4,0,3,2,1:T(8,128)S(1)} %copy.365) | copy-start | bytes 23592964
  21.1 20.3 %collective-permute-start = (f32[1,11,128,128]{3,2,0,1:T(8,128)S(1)}, f32[1,11,128,128]{3,2,0,1:T(8,128)S(1)}, u32[]{:S(2)}, u32[]{:S(2)}) collective-permute-start(f32[1,11,128,128]{3,2,0,1:T(8,128)S(1)} %get-tuple-element.8), channel_id=1, source_target_pairs={{0,1},{2,3},{4,5},{6,7},{8,9},{10,11},{12,13},{14,15},{16,17},{18,... | collective-permute-start | bytes 2162696 | tf_op jit(solution)/shard_map/ppermute | solution.py:14
  26.1 19.5 %collective-permute-start.1 = (f32[1,11,128,128]{3,2,0,1:T(8,128)S(1)}, f32[1,11,128,128]{3,2,0,1:T(8,128)S(1)}, u32[]{:S(2)}, u32[]{:S(2)}) collective-permute-start(f32[1,11,128,128]{3,2,0,1:T(8,128)S(1)} %get-tuple-element.9), channel_id=1, source_target_pairs={{1,0},{3,2},{5,4},{7,6},{9,8},{11,10},{13,12},{15,14},{17,16},{19,... | collective-permute-start | bytes 2162696 | tf_op jit(solution)/shard_map/ppermute | solution.py:17
  49.3 158.3 %collective-permute-start.2 = (f32[42,1,1,3,128,128]{5,4,0,3,2,1:T(8,128)}, f32[42,1,1,3,128,128]{5,4,0,3,2,1:T(8,128)}, u32[]{:S(2)}, u32[]{:S(2)}) collective-permute-start(f32[42,1,1,3,128,128]{5,4,0,3,2,1:T(8,128)} %fusion.7), channel_id=1, source_target_pairs={{0,8},{8,16},{16,24},{24,0},{1,9},{9,17},{17,25},{25,1},{2,10},{10... | collective-permute-start | bytes 24772616 | tf_op jit(solution)/shard_map/ppermute | solution.py:55
  49.9 46.9 %slice-start.2 = ((s8[20971520]{0:T(1024)(128)(4,1)}), s8[4194304]{0:T(1024)(128)(4,1)S(1)}, s32[]{:S(2)}) async-start(s8[20971520]{0:T(1024)(128)(4,1)} %bitcast.492), calls=%async_computation.3 | async-start | bytes 8388608
  49.9 46.8 %slice-start.3 = ((s8[20971520]{0:T(1024)(128)(4,1)}), s8[4194304]{0:T(1024)(128)(4,1)S(1)}, s32[]{:S(2)}) async-start(s8[20971520]{0:T(1024)(128)(4,1)} %bitcast.492), calls=%async_computation.4 | async-start | bytes 8388608
  49.9 46.8 %slice-start.4 = ((s8[20971520]{0:T(1024)(128)(4,1)}), s8[4194304]{0:T(1024)(128)(4,1)S(1)}, s32[]{:S(2)}) async-start(s8[20971520]{0:T(1024)(128)(4,1)} %bitcast.492), calls=%async_computation.5 | async-start | bytes 8388608
  70.8 33.7 %slice-start.12 = ((s8[7864320]{0:T(1024)(128)(4,1)}), s8[4194304]{0:T(1024)(128)(4,1)S(1)}, s32[]{:S(2)}) async-start(s8[7864320]{0:T(1024)(128)(4,1)} %bitcast.496), calls=%async_computation.13 | async-start | bytes 8388608
  78.7 18.0 %slice-start.5 = ((s8[20971520]{0:T(1024)(128)(4,1)}), s8[4194304]{0:T(1024)(128)(4,1)S(1)}, s32[]{:S(2)}) async-start(s8[20971520]{0:T(1024)(128)(4,1)} %bitcast.492), calls=%async_computation.6 | async-start | bytes 8388608
  78.7 18.0 %slice-start.6 = ((s8[20971520]{0:T(1024)(128)(4,1)}), s8[4194304]{0:T(1024)(128)(4,1)S(1)}, s32[]{:S(2)}) async-start(s8[20971520]{0:T(1024)(128)(4,1)} %bitcast.492), calls=%async_computation.7 | async-start | bytes 8388608
  78.7 25.8 %slice-start.13 = ((s8[7864320]{0:T(1024)(128)(4,1)}), s8[3670016]{0:T(1024)(128)(4,1)S(1)}, s32[]{:S(2)}) async-start(s8[7864320]{0:T(1024)(128)(4,1)} %bitcast.496), calls=%async_computation.14 | async-start | bytes 7340032
  190.1 223.0 %collective-permute-start.3 = (f32[42,1,1,3,128,128]{5,4,0,3,2,1:T(8,128)}, f32[42,1,1,3,128,128]{5,4,0,3,2,1:T(8,128)}, u32[]{:S(2)}, u32[]{:S(2)}) collective-permute-start(f32[42,1,1,3,128,128]{5,4,0,3,2,1:T(8,128)} %fusion.7), channel_id=1, source_target_pairs={{0,24},{8,0},{16,8},{24,16},{1,25},{9,1},{17,9},{25,17},{2,26},{10... | collective-permute-start | bytes 24772616 | tf_op jit(solution)/shard_map/ppermute | solution.py:60
  207.6 226.4 %collective-permute-start.4 = (f32[42,1,1,3,128,128]{5,4,0,3,2,1:T(8,128)}, f32[42,1,1,3,128,128]{5,4,0,3,2,1:T(8,128)}, u32[]{:S(2)}, u32[]{:S(2)}) collective-permute-start(f32[42,1,1,3,128,128]{5,4,0,3,2,1:T(8,128)} %collective-permute-done.2), channel_id=1, source_target_pairs={{0,8},{8,16},{16,24},{24,0},{1,9},{9,17},{17,25},{25,1},{2,10},{10... | collective-permute-start | bytes 24772616 | tf_op jit(solution)/shard_map/ppermute | solution.py:55
  255.5 24.5 %slice-start.7 = ((s8[20971520]{0:T(1024)(128)(4,1)}), s8[4194304]{0:T(1024)(128)(4,1)S(1)}, s32[]{:S(2)}) async-start(s8[20971520]{0:T(1024)(128)(4,1)} %bitcast.494), calls=%async_computation.8 | async-start | bytes 8388608
  255.5 24.5 %slice-start.8 = ((s8[20971520]{0:T(1024)(128)(4,1)}), s8[4194304]{0:T(1024)(128)(4,1)S(1)}, s32[]{:S(2)}) async-start(s8[20971520]{0:T(1024)(128)(4,1)} %bitcast.494), calls=%async_computation.9 | async-start | bytes 8388608
  255.5 24.5 %slice-start.9 = ((s8[20971520]{0:T(1024)(128)(4,1)}), s8[4194304]{0:T(1024)(128)(4,1)S(1)}, s32[]{:S(2)}) async-start(s8[20971520]{0:T(1024)(128)(4,1)} %bitcast.494), calls=%async_computation.10 | async-start | bytes 8388608
  255.5 24.5 %slice-start.10 = ((s8[20971520]{0:T(1024)(128)(4,1)}), s8[4194304]{0:T(1024)(128)(4,1)S(1)}, s32[]{:S(2)}) async-start(s8[20971520]{0:T(1024)(128)(4,1)} %bitcast.494), calls=%async_computation.11 | async-start | bytes 8388608
  280.1 15.5 %slice-start = ((s8[7864320]{0:T(1024)(128)(4,1)}), s8[4194304]{0:T(1024)(128)(4,1)S(1)}, s32[]{:S(2)}) async-start(s8[7864320]{0:T(1024)(128)(4,1)} %bitcast.476), calls=%async_computation.1 | async-start | bytes 8388608
  623.1 34.2 %slice-start.14 = ((s8[10485760]{0:T(1024)(128)(4,1)}), s8[2097152]{0:T(1024)(128)(4,1)S(1)}, s32[]{:S(2)}) async-start(s8[10485760]{0:T(1024)(128)(4,1)} %bitcast.498), calls=%async_computation.15 | async-start | bytes 4194304
  623.1 34.2 %slice-start.15 = ((s8[10485760]{0:T(1024)(128)(4,1)}), s8[4194304]{0:T(1024)(128)(4,1)S(1)}, s32[]{:S(2)}) async-start(s8[10485760]{0:T(1024)(128)(4,1)} %bitcast.498), calls=%async_computation.16 | async-start | bytes 8388608
  637.8 19.4 %slice-start.16 = ((s8[10485760]{0:T(1024)(128)(4,1)}), s8[4194304]{0:T(1024)(128)(4,1)S(1)}, s32[]{:S(2)}) async-start(s8[10485760]{0:T(1024)(128)(4,1)} %bitcast.498), calls=%async_computation.17 | async-start | bytes 8388608
  637.8 19.4 %copy-start.4 = (f32[40,128,128,1]{1,2,3,0:T(8,128)S(1)}, f32[40,128,128,1]{1,2,3,0:T(8,128)}, u32[]{:S(2)}) copy-start(f32[40,128,128,1]{1,2,3,0:T(8,128)} %fusion.4) | copy-start | bytes 7864324
  (6 other events, 57.1 us)
Sparse Core Ops, SparseCore 0:
  15.4 529.8 all-gather.1
